TPU v7x, 128 devices: a whole 4x4x4 slice. The times are simulated.
128 devices in a mesh: leaf: 64 (over y_hi, x, z, core), rhs: 2 (over y_lo).
Axes of the slice: x: 4, y: 4 (y_hi: 2, y_lo: 2; y = y_hi * 2 + y_lo), z: 4, core: 2. Of those that a mesh axis runs over, the one named last changes fastest.
Arguments:
- rhs: bfloat16 [524288, 512], P('leaf', 'rhs'), may hold values from -6 to 6
- source_basis: bfloat16 [4096, 128, 128], P('leaf', None, 'rhs'), may hold values from -0.5 to 0.5
- target_basis: bfloat16 [4096, 128, 128], P('leaf', None, 'rhs'), may hold values from -0.5 to 0.5
- near_blocks: bfloat16 [4096, 2, 128, 128], P('leaf', None, None, 'rhs'), may hold values from -0.375 to 0.375
- near_offsets: int32 [4096, 2], P('leaf'), may hold values from -2 to 2
- source_values: bfloat16 [3, 2048, 2, 2, 128, 128], P(None, 'leaf', None, None, 'rhs'), may hold values from -0.375 to 0.375
- source_scales: float32 [3, 2048, 2, 2, 128], P(None, 'leaf'), may hold values from 0.2 to 2
- target_values: bfloat16 [3, 2048, 2, 2, 128, 128], P(None, 'leaf', None, None, 'rhs'), may hold values from -0.375 to 0.375
- target_scales: float32 [3, 2048, 2, 2, 128], P(None, 'leaf'), may hold values from 0.2 to 2
Outputs:
- product: bfloat16 [524288, 512], P('leaf', 'rhs')
All inputs are finite; a program needn't handle non-finite values.
Results may differ from a plain program's by a relative error of at most 0.01.
Values may be sent and summed in bfloat16 or wider, within the bound.
A program may use at most 192 MiB of HBM per device.

v0:
```python
import jax
import jax.numpy as jnp
from jax import lax
from jax.sharding import PartitionSpec as P

REACH = 2
SRC_LEVELS = 3
TGT_LEVELS = 3


def padded_2(cells, sides, width):
    for axis, dim in sides:
        count = lax.axis_size(axis)
        ends = count - 1
        head = lax.slice_in_dim(cells, 0, width, axis=dim)
        tail = lax.slice_in_dim(cells, cells.shape[dim] - width, cells.shape[dim], axis=dim)
        cells = jnp.concatenate(
            [
                lax.ppermute(tail, axis, [(i, (i + 1) % count) for i in range(ends)]),
                cells,
                lax.ppermute(head, axis, [((i + 1) % count, i) for i in range(ends)]),
            ],
            axis=dim,
        )
    return cells


def dequantize(values, scales):
    return (values.astype(jnp.float32) * scales[..., None, :]).astype(jnp.bfloat16)


def butterfly_level(coefficients, blocks, bit_index):
    box_total, columns, rank = coefficients.shape
    outputs = blocks.shape[-2]
    low_span = 2**bit_index
    high_span = box_total // (2 * low_span)
    inputs = coefficients.reshape(high_span, 2, low_span, columns, rank)
    matrices = blocks.reshape(high_span, low_span, 2, 2, outputs, rank)
    mixed = jnp.einsum("hclnr,hlocsr->holns", inputs, matrices, preferred_element_type=jnp.float32)
    return mixed.reshape(box_total, columns, outputs).astype(jnp.bfloat16)


def apply_level(coefficients, scales, bit_index, gathered):
    return butterfly_level(coefficients, dequantize(gathered, scales), bit_index)


def on_device(
    rhs,
    source_basis,
    target_basis,
    near_blocks,
    near_offsets,
    source_values,
    source_scales,
    target_values,
    target_scales,
):
    box_count = source_basis.shape[0]
    box_rows = source_basis.shape[1]
    columns = rhs.shape[1]
    rhs_boxes = rhs.reshape(box_count, box_rows, columns)
    basis_in, basis_out, near_full = (
        lax.all_gather(source_basis, "rhs", axis=2, tiled=True),
        lax.all_gather(target_basis, "rhs", axis=2, tiled=True),
        lax.all_gather(near_blocks, "rhs", axis=3, tiled=True),
    )
    source_tables, target_tables = (
        lax.all_gather(source_values, "rhs", axis=4, tiled=True),
        lax.all_gather(target_values, "rhs", axis=4, tiled=True),
    )
    coefficients = jnp.einsum(
        "bmc,bmr->bcr", rhs_boxes, basis_in, preferred_element_type=jnp.float32
    ).astype(jnp.bfloat16)
    for level_index in range(SRC_LEVELS):
        coefficients = apply_level(
            coefficients, source_scales[level_index], level_index, source_tables[level_index]
        )
    padded = padded_2(rhs_boxes, (("leaf", 0),), REACH)
    source_index = jnp.arange(box_count, dtype=jnp.int32)[:, None] + REACH + near_offsets
    selected = jnp.take(padded, source_index, axis=0)
    near_field = jnp.einsum(
        "bkmn,bknc->bmc", near_full, selected, preferred_element_type=jnp.float32
    )
    row_coefficients = lax.all_to_all(coefficients, "leaf", split_axis=0, concat_axis=0, tiled=True)
    for level_index in range(TGT_LEVELS):
        row_coefficients = apply_level(
            row_coefficients, target_scales[level_index], level_index, target_tables[level_index]
        )
    far_field = jnp.einsum(
        "bmr,bcr->bmc", basis_out, row_coefficients, preferred_element_type=jnp.float32
    )
    return (far_field + near_field).astype(jnp.bfloat16).reshape(box_count * box_rows, columns)


def solution(mesh):
    placed = (
        P("leaf", "rhs"),
        P("leaf", None, "rhs"),
        P("leaf", None, "rhs"),
        P("leaf", None, None, "rhs"),
        P("leaf", None),
        P(None, "leaf", None, None, "rhs", None),
        P(None, "leaf", None, None, None),
        P(None, "leaf", None, None, "rhs", None),
        P(None, "leaf", None, None, None),
    )
    return jax.shard_map(
        on_device, mesh=mesh, in_specs=placed, out_specs=P("leaf", "rhs"), check_vma=False
    )
```

profile of v0, /device:TPU:1, one launch (start us, length us, event | category | flops | bytes accessed | tf_op | source)
XLA Modules:
  0.0 526.6 jit_solution(11540010097013420315)
XLA Ops:
  6.5 0.0 all-gather.10.cloned.1.call-start
  6.5 0.7 all-gather.10.cloned.1.call-update
  7.3 0.0 all-gather.8.cloned.1.call-start
  7.3 0.7 all-gather.8.cloned.1.call-update
  8.0 0.0 copy-start.2
  8.0 0.0 all-gather.6.cloned.1.call-start
  8.1 0.7 all-gather.6.cloned.1.call-update
  8.8 0.2 copy-done.2
  9.0 38.7 %all-gather.10.cloned.1.call-done = bf16[64,128,128]{1,2,0:T(8,128)(2,1)} async-done(((bf16[64,128,64]{1,2,0:T(8,128)(2,1)}), bf16[64,128,128]{1,2,0:T(8,128)(2,1)}) %all-gather.10.cloned.1.call-update) | async-done | bytes 2097168 | tf_op jit(solution)/shard_map/all_gather | solution.py:63
  47.7 6.2 %convolution_convert_fusion = bf16[64,256,128]{2,1,0:T(8,128)(2,1)} fusion(bf16[64,128,256]{2,1,0:T(8,128)(2,1)} %bitcast.118, bf16[64,128,128]{1,2,0:T(8,128)(2,1)} %all-gather.10.cloned.1.call-done), kind=kOutput, calls=%fused_computation.48 | convolution fusion | flops 538968064 | bytes 10485760 | tf_op jit(solution)/shard_map/bmc,bmr->bcr/dot_general | solution.py:71
  53.9 151.5 %all-gather.8.cloned.1.call-done = bf16[3,32,2,2,128,128]{5,4,3,2,1,0:T(8,128)(2,1)} async-done(((bf16[3,32,2,2,64,128]{5,4,3,2,1,0:T(8,128)(2,1)}), bf16[3,32,2,2,128,128]{5,4,3,2,1,0:T(8,128)(2,1)}) %all-gather.8.cloned.1.call-update) | async-done | bytes 12582928 | tf_op jit(solution)/shard_map/all_gather | solution.py:68
  205.4 5.4 %fusion.61 = (bf16[1,32,2,2,128,128]{5,4,3,2,1,0:T(8,128)(2,1)}, bf16[1,32,2,2,128,128]{5,4,3,2,1,0:T(8,128)(2,1)S(1)}) fusion(bf16[3,32,2,2,128,128]{5,4,3,2,1,0:T(8,128)(2,1)} %all-gather.8.cloned.1.call-done), kind=kLoop, calls=%fused_computation.57 | loop fusion | bytes 16777216 | tf_op jit(solution)/shard_map/slice | solution.py:76
  210.8 0.8 copy-done
  211.5 3.5 bitcast_convert_fusion.5
  215.0 3.6 fusion.10
  218.6 6.9 %copy.17 = bf16[16,2,2,256,128]{4,3,2,1,0:T(8,128)(2,1)} copy(bf16[16,2,2,256,128]{3,4,1,2,0:T(8,128)(2,1)} %fusion.10) | data formatting | bytes 8388608 | tf_op jit(solution)/shard_map/convert_element_type | solution.py:40
  225.6 7.4 %fusion.11 = bf16[8,2,4,256,128]{3,4,1,2,0:T(8,128)(2,1)} fusion(bf16[8,2,4,256,128,1]{4,3,2,1,0,5:T(8,128)(2,1)} %bitcast.123, bf16[8,4,2,2,128,128]{5,4,3,2,1,0:T(8,128)(2,1)} %bitcast.126, f32[8,4,2,2,128]{4,3,2,1,0:T(2,128)S(1)} %bitcast.133), kind=kOutput, calls=%fused_computation.26 | convolution fusion | flops 1082130432 | bytes 12648448 | tf_op jit(solution)/shard_map/hclnr,hlocsr->holns/dot_general | solution.py:39
  233.0 6.5 %copy.19 = bf16[8,2,4,256,128]{4,3,2,1,0:T(8,128)(2,1)} copy(bf16[8,2,4,256,128]{3,4,1,2,0:T(8,128)(2,1)} %fusion.11) | data formatting | bytes 8388608 | tf_op jit(solution)/shard_map/convert_element_type | solution.py:40
  239.5 10.7 %all-to-all-start = ((bf16[64,256,128]{2,1,0:T(8,128)(2,1)}), bf16[64,256,128]{2,1,0:T(8,128)(2,1)}, u32[]{:S(2)}, u32[]{:S(2)}) async-start(bf16[64,256,128]{2,1,0:T(8,128)(2,1)} %bitcast.121), calls=%async_computation | async-start | bytes 8388608 | tf_op jit(solution)/shard_map/all_to_all | solution.py:84
  250.3 0.0 all-gather.12.cloned.1.call-start
  250.3 0.5 all-gather.12.cloned.1.call-update
  250.8 0.0 all-gather.14.cloned.1.call-start
  250.9 0.5 all-gather.14.cloned.1.call-update
  251.4 1.0 fusion.62
  252.4 3.5 collective-permute-start
  256.0 2.1 collective-permute-start.1
  258.1 0.0 copy-done.3
  258.1 0.0 copy-done.4
  258.1 0.1 copy.25
  258.2 0.1 reshape.106
  258.4 0.1 copy.24
  258.5 13.0 %collective-permute-done = bf16[2,128,256]{2,1,0:T(8,128)(2,1)S(1)} collective-permute-done((bf16[2,128,256]{2,1,0:T(8,128)(2,1)S(1)}, bf16[2,128,256]{2,1,0:T(8,128)(2,1)S(1)}, u32[]{:S(2)}, u32[]{:S(2)}) %collective-permute-start) | collective-permute-done | bytes 131104 | tf_op jit(solution)/shard_map/ppermute | solution.py:19
  271.5 2.2 collective-permute-done.1
  273.7 4.0 pad_maximum_fusion
  277.7 8.8 %gather_fusion = bf16[128,128,256]{2,1,0:T(8,128)(2,1)} fusion(bf16[68,128,256]{2,1,0:T(8,128)(2,1)} %pad_maximum_fusion, s32[1024]{0:T(1024)S(1)} %pad_clamp_fusion), kind=kCustom, calls=%fused_computation | custom fusion | bytes 16777728 | tf_op jit(solution)/shard_map/jit(_take)/gather | solution.py:80
  286.5 121.5 %all-gather.6.cloned.1.call-done = bf16[3,32,2,2,128,128]{5,4,3,2,1,0:T(8,128)(2,1)} async-done(((bf16[3,32,2,2,64,128]{5,4,3,2,1,0:T(8,128)(2,1)}), bf16[3,32,2,2,128,128]{5,4,3,2,1,0:T(8,128)(2,1)}) %all-gather.6.cloned.1.call-update) | async-done | bytes 12582928 | tf_op jit(solution)/shard_map/all_gather | solution.py:69
  408.0 6.2 %fusion.60 = (bf16[1,32,2,2,128,128]{5,4,3,2,1,0:T(8,128)(2,1)}, bf16[1,32,2,2,128,128]{5,4,3,2,1,0:T(8,128)(2,1)}) fusion(bf16[3,32,2,2,128,128]{5,4,3,2,1,0:T(8,128)(2,1)} %all-gather.6.cloned.1.call-done), kind=kLoop, calls=%fused_computation.56 | loop fusion | bytes 16777216 | tf_op jit(solution)/shard_map/slice | solution.py:87
  414.2 0.0 all-to-all-done
  414.2 4.9 bitcast_convert_fusion.2
  419.1 0.0 copy-done.1
  419.1 3.2 fusion.12
  422.4 6.6 %copy.21 = bf16[16,2,2,256,128]{4,3,2,1,0:T(8,128)(2,1)} copy(bf16[16,2,2,256,128]{3,4,1,2,0:T(8,128)(2,1)} %fusion.12) | data formatting | bytes 8388608 | tf_op jit(solution)/shard_map/convert_element_type | solution.py:40
  429.0 6.7 %fusion.13 = bf16[8,2,4,256,128]{3,4,1,2,0:T(8,128)(2,1)} fusion(bf16[8,2,4,256,128,1]{4,3,2,1,0,5:T(8,128)(2,1)} %bitcast.124, bf16[8,4,2,2,128,128]{5,4,3,2,1,0:T(8,128)(2,1)} %bitcast.125, f32[8,4,2,2,128]{4,3,2,1,0:T(2,128)S(1)} %bitcast.131), kind=kOutput, calls=%fused_computation.28 | convolution fusion | flops 1082130432 | bytes 12648448 | tf_op jit(solution)/shard_map/hclnr,hlocsr->holns/dot_general | solution.py:39
  435.7 6.4 %copy.23 = bf16[8,2,4,256,128]{4,3,2,1,0:T(8,128)(2,1)} copy(bf16[8,2,4,256,128]{3,4,1,2,0:T(8,128)(2,1)} %fusion.13) | data formatting | bytes 8388608 | tf_op jit(solution)/shard_map/convert_element_type | solution.py:40
  442.1 6.1 %all-gather.12.cloned.1.call-done = bf16[64,128,128]{1,2,0:T(8,128)(2,1)} async-done(((bf16[64,128,64]{1,2,0:T(8,128)(2,1)}), bf16[64,128,128]{1,2,0:T(8,128)(2,1)}) %all-gather.12.cloned.1.call-update) | async-done | bytes 2097168 | tf_op jit(solution)/shard_map/all_gather | solution.py:64
  448.3 7.4 %fusion.65 = f32[64,256,128]{1,2,0:T(8,128)} fusion(bf16[64,256,128]{2,1,0:T(8,128)(2,1)} %bitcast.120, bf16[64,128,128]{1,2,0:T(8,128)(2,1)} %all-gather.12.cloned.1.call-done), kind=kOutput, calls=%fused_computation.61 | convolution fusion | flops 536870912 | bytes 14680064 | tf_op jit(solution)/shard_map/bmr,bcr->bmc/dot_general | solution.py:89
  455.7 54.3 %all-gather.14.cloned.1.call-done = bf16[64,2,128,128]{2,3,1,0:T(8,128)(2,1)} async-done(((bf16[64,2,128,64]{2,3,1,0:T(8,128)(2,1)}), bf16[64,2,128,128]{2,3,1,0:T(8,128)(2,1)}) %all-gather.14.cloned.1.call-update) | async-done | bytes 4194320 | tf_op jit(solution)/shard_map/all_gather | solution.py:65
  510.0 10.1 %fusion.6 = bf16[64,256,128]{1,2,0:T(8,128)(2,1)} fusion(f32[64,256,128]{1,2,0:T(8,128)} %fusion.65, bf16[64,2,128,128]{2,3,1,0:T(8,128)(2,1)} %all-gather.14.cloned.1.call-done, bf16[64,2,128,256]{3,2,1,0:T(8,128)(2,1)} %bitcast.117, pred[64,2]{1,0:T(8,128)(4,1)S(1)} %copy.24), kind=kOutput, calls=%fused_computation.14 | convolution fusion | flops 1082130432 | bytes 25165952 | tf_op jit(solution)/shard_map/bkmn,bknc->bmc/dot_general | solution.py:81
  (9 shorter events, 0.1 us)
Async XLA Ops:
  6.5 41.1 %all-gather.10.cloned.1.call-start = ((), (), s32[]{:S(2)}) async-start(), calls=%async_computation.3 | async-start | bytes 3145728 | tf_op jit(solution)/shard_map/all_gather | solution.py:63
  7.3 198.1 %all-gather.8.cloned.1.call-start = ((), (), s32[]{:S(2)}) async-start(), calls=%async_computation.2 | async-start | bytes 18874368 | tf_op jit(solution)/shard_map/all_gather | solution.py:68
  8.0 0.9 copy-start.2
  8.0 400.0 %all-gather.6.cloned.1.call-start = ((), (), s32[]{:S(2)}) async-start(), calls=%async_computation.1 | async-start | bytes 18874368 | tf_op jit(solution)/shard_map/all_gather | solution.py:69
  205.4 6.2 %copy-start = (bf16[64,256,128]{2,1,0:T(8,128)(2,1)S(1)}, bf16[64,256,128]{2,1,0:T(8,128)(2,1)}, u32[]{:S(2)}) copy-start(bf16[64,256,128]{2,1,0:T(8,128)(2,1)} %convolution_convert_fusion) | copy-start | bytes 12582916
  239.5 18.6 %copy-start.3 = (f32[3,32,2,2,128]{4,3,2,1,0:T(2,128)S(1)}, f32[3,32,2,2,128]{4,3,2,1,0:T(2,128)}, u32[]{:S(2)}) copy-start(f32[3,32,2,2,128]{4,3,2,1,0:T(2,128)} %param.17) | copy-start | bytes 589828
  239.5 18.6 %copy-start.4 = (s32[64,2]{0,1:T(2,128)S(1)}, s32[64,2]{0,1:T(2,128)}, u32[]{:S(2)}) copy-start(s32[64,2]{0,1:T(2,128)} %param.13) | copy-start | bytes 1540
  239.5 174.7 %all-to-all-start = ((bf16[64,256,128]{2,1,0:T(8,128)(2,1)}), bf16[64,256,128]{2,1,0:T(8,128)(2,1)}, u32[]{:S(2)}, u32[]{:S(2)}) async-start(bf16[64,256,128]{2,1,0:T(8,128)(2,1)} %bitcast.121), calls=%async_computation | async-start | bytes 8388608 | tf_op jit(solution)/shard_map/all_to_all | solution.py:84
  250.3 198.0 %all-gather.12.cloned.1.call-start = ((), (), s32[]{:S(2)}) async-start(), calls=%async_computation.4 | async-start | bytes 3145728 | tf_op jit(solution)/shard_map/all_gather | solution.py:64
  250.8 259.2 %all-gather.14.cloned.1.call-start = ((), (), s32[]{:S(2)}) async-start(), calls=%async_computation.5 | async-start | bytes 6291456 | tf_op jit(solution)/shard_map/all_gather | solution.py:65
  252.4 19.1 %collective-permute-start = (bf16[2,128,256]{2,1,0:T(8,128)(2,1)S(1)}, bf16[2,128,256]{2,1,0:T(8,128)(2,1)S(1)}, u32[]{:S(2)}, u32[]{:S(2)}) collective-permute-start(bf16[2,128,256]{2,1,0:T(8,128)(2,1)S(1)} %bitcast.130), channel_id=1, source_target_pairs={{0,2},{2,4},{4,6},{6,8},{8,10},{10,12},{12,14},{14,16},{16,18},{18... | collective-permute-start | bytes 393224 | tf_op jit(solution)/shard_map/ppermute | solution.py:19
  256.0 17.8 %collective-permute-start.1 = (bf16[2,128,256]{2,1,0:T(8,128)(2,1)S(1)}, bf16[2,128,256]{2,1,0:T(8,128)(2,1)S(1)}, u32[]{:S(2)}, u32[]{:S(2)}) collective-permute-start(bf16[2,128,256]{2,1,0:T(8,128)(2,1)S(1)} %bitcast.129), channel_id=1, source_target_pairs={{2,0},{4,2},{6,4},{8,6},{10,8},{12,10},{14,12},{16,14},{18,16},{20... | collective-permute-start | bytes 393224 | tf_op jit(solution)/shard_map/ppermute | solution.py:21
  414.2 4.9 copy-start.1
Sparse Core Ops, SparseCore 0:
  9.0 38.6 all-gather.9
  49.3 155.9 all-gather.7
  207.0 200.9 all-gather.5
  409.5 38.7 all-gather.11
  449.8 60.2 all-gather.13
where the time goes:
time: 528 us; the launch traced here: 527 us
  waiting for transfers between devices  391 us (74%)
  matrix products  53.1 us (10%)
  local copies, waits for them, and re-layouts  49.3 us (9%)
  starting transfers between devices  16.5 us (3%)
  between operations  13.3 us (3%)
    all_gather x1, waiting for transfers between devices, on_device(): lax.all_gather(source_values, 'rhs', axis=4, tiled=True)  152 us
    all_gather x1, waiting for transfers between devices, on_device(): lax.all_gather(target_values, 'rhs', axis=4, tiled=True)  121 us
    all_gather x1, waiting for transfers between devices, on_device(): lax.all_gather(near_blocks, 'rhs', axis=3, tiled=True)  54.3 us
    all_gather x1, waiting for transfers between devices, on_device(): lax.all_gather(source_basis, 'rhs', axis=2, tiled=True)  38.7 us
    dot_general x6, matrix products, butterfly_level(): jnp.einsum('hclnr,hlocsr->holns', inputs, matrices, preferred_element_typ...  29.3 us
    convert_element_type x4, local copies, waits for them, and re-layouts, butterfly_level(): return mixed.reshape(box_total, columns, outputs).astype(jnp.bfloat16)  26.5 us
    ppermute x1, waiting for transfers between devices, padded_2(): lax.ppermute(tail, axis, [(i, (i + 1) % count) for i in range(ends)])  13 us
    all_to_all x1, starting transfers between devices, on_device(): lax.all_to_all(coefficients, 'leaf', split_axis=0, concat_axis=0, tiled=T...  10.7 us
  transfers between devices with their start and end apart: 8, of which 7 were waited for; matrix products, arithmetic and copies ran while one was open for 18% of the time, Pallas kernels for 0%

commit v1 on v0

--- a/solution.py
+++ b/solution.py
@@ -65,7 +65,9 @@
         lax.all_gather(near_blocks, "rhs", axis=3, tiled=True),
     )
     source_tables, target_tables = (
-        lax.all_gather(source_values, "rhs", axis=4, tiled=True),
+        jnp.concatenate(
+            lax.all_to_all(jnp.stack([source_values] * lax.axis_size("rhs")), "rhs", 0, 0), axis=4
+        ),
         lax.all_gather(target_values, "rhs", axis=4, tiled=True),
     )
     coefficients = jnp.einsum(

time: 528 us -> 483 us (0.915)
  waiting for transfers between devices: 391 us -> 318 us
  other arithmetic: 3.97 us -> 15.1 us
  starting transfers between devices: 16.5 us -> 26 us
  local copies, waits for them, and re-layouts: 49.3 us -> 56.7 us
    all_to_all x0 -> x1, waiting for transfers between devices: none -> 210 us  [on_device(): lax.all_to_all(jnp.stack([source_values] * lax.axis_size('rhs')), 'rhs',...]
    all_gather x1 -> x0, waiting for transfers between devices: 152 us -> none  [on_device(): lax.all_gather(source_values, 'rhs', axis=4, tiled=True)]
    all_gather x1, waiting for transfers between devices: 121 us -> 0.01 us  [on_device(): lax.all_gather(target_values, 'rhs', axis=4, tiled=True)]
    ppermute x1, waiting for transfers between devices: 13 us -> 32.9 us  [padded_2(): lax.ppermute(tail, axis, [(i, (i + 1) % count) for i in range(ends)])]
    all_gather x1, waiting for transfers between devices: 54.3 us -> 37.7 us  [on_device(): lax.all_gather(near_blocks, 'rhs', axis=3, tiled=True)]
    another operation x0 -> x1, other arithmetic: none -> 11 us  [on_device(): jnp.stack([source_values] * lax.axis_size('rhs'))]
    all_to_all x0 -> x1, starting transfers between devices: none -> 8.95 us  [on_device(): lax.all_to_all(jnp.stack([source_values] * lax.axis_size('rhs')), 'rhs',...]
    all_to_all x0 -> x1, local copies, waits for them, and re-layouts: none -> 6.54 us  [on_device(): lax.all_to_all(jnp.stack([source_values] * lax.axis_size('rhs')), 'rhs',...]
  transfers between devices with their start and end apart: 8 -> 8, of which waited for: 7 -> 4; matrix products, arithmetic and copies ran while one was open for 18% -> 24% of each run, Pallas kernels for 0% -> 0%
where the time goes in v1:
time: 483 us; the launch traced here: 482 us
  waiting for transfers between devices  318 us (66%)
  local copies, waits for them, and re-layouts  56.7 us (12%)
  matrix products  52.6 us (11%)
  starting transfers between devices  26 us (5%)
  other arithmetic  15.1 us (3%)
  between operations  13.3 us (3%)
    all_to_all x1, waiting for transfers between devices, on_device(): lax.all_to_all(jnp.stack([source_values] * lax.axis_size('rhs')), 'rhs',...  210 us
    all_gather x1, waiting for transfers between devices, on_device(): lax.all_gather(near_blocks, 'rhs', axis=3, tiled=True)  37.7 us
    all_gather x1, waiting for transfers between devices, on_device(): lax.all_gather(source_basis, 'rhs', axis=2, tiled=True)  35.1 us
    ppermute x1, waiting for transfers between devices, padded_2(): lax.ppermute(tail, axis, [(i, (i + 1) % count) for i in range(ends)])  32.9 us
    dot_general x6, matrix products, butterfly_level(): jnp.einsum('hclnr,hlocsr->holns', inputs, matrices, preferred_element_typ...  28.4 us
    convert_element_type x4, local copies, waits for them, and re-layouts, butterfly_level(): return mixed.reshape(box_total, columns, outputs).astype(jnp.bfloat16)  25.9 us
    all_to_all x1, starting transfers between devices, on_device(): lax.all_to_all(coefficients, 'leaf', split_axis=0, concat_axis=0, tiled=T...  11.2 us
    another operation x1, other arithmetic, on_device(): jnp.stack([source_values] * lax.axis_size('rhs'))  11 us
  transfers between devices with their start and end apart: 8, of which 4 were waited for; matrix products, arithmetic and copies ran while one was open for 24% of the time, Pallas kernels for 0%

profile of v1, /device:TPU:1, one launch (start us, length us, event | category | flops | bytes accessed | tf_op | source)
XLA Modules:
  0.0 481.9 jit_solution(8543133722382979047)
XLA Ops:
  6.5 0.0 all-gather.7.cloned.1.call-start
  6.5 0.7 all-gather.7.cloned.1.call-update
  7.3 0.0 all-gather.5.cloned.1.call-start
  7.3 0.7 all-gather.5.cloned.1.call-update
  8.0 11.0 %pad_maximum_fusion = bf16[2,3,32,2,2,64,128]{6,5,4,3,2,1,0:T(8,128)(2,1)} fusion(bf16[1,3,32,2,2,64,128]{6,5,4,3,2,1,0:T(8,128)(2,1)} %bitcast.123), kind=kLoop, calls=%fused_computation.1 | loop fusion | flops 6291456 | bytes 18874368 | tf_op jit(solution)/shard_map/stack | solution.py:69
  19.0 0.0 copy-start.2
  19.0 8.9 %all-to-all-start = ((bf16[2,3,32,2,2,64,128]{6,5,4,3,2,1,0:T(8,128)(2,1)}), bf16[2,3,32,2,2,64,128]{6,5,4,3,2,1,0:T(8,128)(2,1)}, u32[]{:S(2)}, u32[]{:S(2)}) async-start(bf16[2,3,32,2,2,64,128]{6,5,4,3,2,1,0:T(8,128)(2,1)} %pad_maximum_fusion), calls=%async_computation | async-start | bytes 25165824 | tf_op jit(solution)/shard_map/all_to_all | solution.py:69
  28.0 0.0 copy-done.2
  28.0 35.1 %all-gather.7.cloned.1.call-done = bf16[64,128,128]{1,2,0:T(8,128)(2,1)} async-done(((bf16[64,128,64]{1,2,0:T(8,128)(2,1)}), bf16[64,128,128]{1,2,0:T(8,128)(2,1)}) %all-gather.7.cloned.1.call-update) | async-done | bytes 2097168 | tf_op jit(solution)/shard_map/all_gather | solution.py:63
  63.1 6.2 %convolution_convert_fusion = bf16[64,256,128]{2,1,0:T(8,128)(2,1)} fusion(bf16[64,128,256]{2,1,0:T(8,128)(2,1)} %bitcast.117, bf16[64,128,128]{1,2,0:T(8,128)(2,1)} %all-gather.7.cloned.1.call-done), kind=kOutput, calls=%fused_computation.49 | convolution fusion | flops 538968064 | bytes 10485760 | tf_op jit(solution)/shard_map/bmc,bmr->bcr/dot_general | solution.py:73
  69.3 209.9 %all-to-all-done = bf16[2,3,32,2,2,64,128]{6,5,4,3,2,1,0:T(8,128)(2,1)} async-done(((bf16[2,3,32,2,2,64,128]{6,5,4,3,2,1,0:T(8,128)(2,1)}), bf16[2,3,32,2,2,64,128]{6,5,4,3,2,1,0:T(8,128)(2,1)}, u32[]{:S(2)}, u32[]{:S(2)}) %all-to-all-start) | async-done | bytes 12582944 | tf_op jit(solution)/shard_map/all_to_all | solution.py:69
  279.2 6.5 %copy.77 = bf16[2,3,32,2,2,64,128]{6,5,0,4,3,2,1:T(8,128)(2,1)S(1)} copy(bf16[2,3,32,2,2,64,128]{6,5,4,3,2,1,0:T(8,128)(2,1)} %all-to-all-done) | data formatting | bytes 25165824 | tf_op jit(solution)/shard_map/all_to_all | solution.py:69
  285.7 0.0 copy-start
  285.7 7.9 %fusion.61 = (bf16[1,32,2,2,2,64,128]{6,5,4,3,2,1,0:T(8,128)(2,1)}, bf16[1,32,2,2,2,64,128]{6,5,4,3,2,1,0:T(8,128)(2,1)S(1)}, bf16[1,32,2,2,2,64,128]{6,5,4,3,2,1,0:T(8,128)(2,1)}) fusion(bf16[3,32,2,2,2,64,128]{6,5,4,3,2,1,0:T(8,128)(2,1)S(1)} %bitcast.115), kind=kLoop, calls=%fused_computation.58 | loop fusion | bytes 25165824 | tf_op jit(solution)/shard_map/slice | solution.py:78
  293.6 0.0 copy-done
  293.6 1.3 bitcast_convert_fusion.5
  294.9 5.5 %fusion.10 = bf16[16,2,2,256,128]{3,4,1,2,0:T(8,128)(2,1)} fusion(bf16[16,2,2,256,128,1]{3,4,2,1,0,5:T(8,128)(2,1)S(1)} %bitcast.124, bf16[16,2,2,2,128,128]{5,4,3,2,1,0:T(8,128)(2,1)} %bitcast.130, f32[16,2,2,2,128]{4,3,2,1,0:T(2,128)S(1)} %bitcast.136), kind=kOutput, calls=%fused_computation.27 | convolution fusion | flops 1082130432 | bytes 12648448 | tf_op jit(solution)/shard_map/hclnr,hlocsr->holns/dot_general | solution.py:39
  300.4 6.4 %copy.29 = bf16[16,2,2,256,128]{4,3,2,1,0:T(8,128)(2,1)} copy(bf16[16,2,2,256,128]{3,4,1,2,0:T(8,128)(2,1)} %fusion.10) | data formatting | bytes 8388608 | tf_op jit(solution)/shard_map/convert_element_type | solution.py:40
  306.7 6.8 %fusion.11 = bf16[8,2,4,256,128]{3,4,1,2,0:T(8,128)(2,1)} fusion(bf16[8,2,4,256,128,1]{4,3,2,1,0,5:T(8,128)(2,1)} %bitcast.125, bf16[8,4,2,2,128,128]{5,4,3,2,1,0:T(8,128)(2,1)} %bitcast.128, f32[8,4,2,2,128]{4,3,2,1,0:T(2,128)S(1)} %bitcast.135), kind=kOutput, calls=%fused_computation.28 | convolution fusion | flops 1082130432 | bytes 12648448 | tf_op jit(solution)/shard_map/hclnr,hlocsr->holns/dot_general | solution.py:39
  313.5 6.4 %copy.31 = bf16[8,2,4,256,128]{4,3,2,1,0:T(8,128)(2,1)} copy(bf16[8,2,4,256,128]{3,4,1,2,0:T(8,128)(2,1)} %fusion.11) | data formatting | bytes 8388608 | tf_op jit(solution)/shard_map/convert_element_type | solution.py:40
  320.0 11.2 %all-to-all-start.1 = ((bf16[64,256,128]{2,1,0:T(8,128)(2,1)}), bf16[64,256,128]{2,1,0:T(8,128)(2,1)}, u32[]{:S(2)}, u32[]{:S(2)}) async-start(bf16[64,256,128]{2,1,0:T(8,128)(2,1)} %bitcast.121), calls=%async_computation.1 | async-start | bytes 8388608 | tf_op jit(solution)/shard_map/all_to_all | solution.py:86
  331.2 0.0 all-gather.9.cloned.1.call-start
  331.3 0.7 all-gather.9.cloned.1.call-update
  331.9 0.0 all-gather.11.cloned.1.call-start
  332.0 0.5 all-gather.11.cloned.1.call-update
  332.5 1.0 fusion.62
  333.5 3.5 collective-permute-start
  337.1 2.1 collective-permute-start.1
  339.2 0.0 copy-done.3
  339.2 0.0 copy-done.4
  339.2 0.1 copy.37
  339.3 0.1 reshape.117
  339.5 0.1 copy.36
  339.6 32.9 %collective-permute-done = bf16[2,128,256]{2,1,0:T(8,128)(2,1)S(1)} collective-permute-done((bf16[2,128,256]{2,1,0:T(8,128)(2,1)S(1)}, bf16[2,128,256]{2,1,0:T(8,128)(2,1)S(1)}, u32[]{:S(2)}, u32[]{:S(2)}) %collective-permute-start) | collective-permute-done | bytes 131104 | tf_op jit(solution)/shard_map/ppermute | solution.py:19
  372.5 0.0 collective-permute-done.1
  372.5 4.1 pad_maximum_fusion.1
  376.6 8.8 %gather_fusion = bf16[128,128,256]{2,1,0:T(8,128)(2,1)} fusion(bf16[68,128,256]{2,1,0:T(8,128)(2,1)} %pad_maximum_fusion.1, s32[1024]{0:T(1024)S(1)} %pad_clamp_fusion), kind=kCustom, calls=%fused_computation | custom fusion | bytes 16777728 | tf_op jit(solution)/shard_map/jit(_take)/gather | solution.py:82
  385.4 6.2 %fusion.60 = (bf16[1,32,2,2,128,128]{5,4,3,2,1,0:T(8,128)(2,1)}, bf16[1,32,2,2,128,128]{5,4,3,2,1,0:T(8,128)(2,1)}) fusion(bf16[3,32,2,2,128,128]{5,4,3,2,1,0:T(8,128)(2,1)} %all-gather.5.cloned.1.call-done), kind=kLoop, calls=%fused_computation.57 | loop fusion | bytes 16777216 | tf_op jit(solution)/shard_map/slice | solution.py:89
  391.6 0.0 all-to-all-done.1
  391.6 4.9 %bitcast_convert_fusion.2 = bf16[32,2,128,256]{3,2,1,0:T(8,128)(2,1)S(1)} fusion(bf16[32,2,256,128,1]{3,2,1,4,0:T(8,128)(2,1)} %bitcast.35, bf16[3,32,2,2,128,128]{5,4,3,2,1,0:T(8,128)(2,1)} %all-gather.5.cloned.1.call-done, f32[32,2,2,128]{3,2,1,0:T(2,128)S(1)} %get-tuple-element.15), kind=kOutput, calls=%fused_computation.19 | convolution fusion | flops 1082130432 | bytes 12648448 | tf_op jit(solution)/shard_map/hclnr,hlocsr->holns/dot_general | solution.py:39
  396.5 0.0 copy-done.1
  396.5 3.2 fusion.12
  399.7 6.5 %copy.33 = bf16[16,2,2,256,128]{4,3,2,1,0:T(8,128)(2,1)} copy(bf16[16,2,2,256,128]{3,4,1,2,0:T(8,128)(2,1)} %fusion.12) | data formatting | bytes 8388608 | tf_op jit(solution)/shard_map/convert_element_type | solution.py:40
  406.2 6.7 %fusion.13 = bf16[8,2,4,256,128]{3,4,1,2,0:T(8,128)(2,1)} fusion(bf16[8,2,4,256,128,1]{4,3,2,1,0,5:T(8,128)(2,1)} %bitcast.126, bf16[8,4,2,2,128,128]{5,4,3,2,1,0:T(8,128)(2,1)} %bitcast.127, f32[8,4,2,2,128]{4,3,2,1,0:T(2,128)S(1)} %bitcast.133), kind=kOutput, calls=%fused_computation.30 | convolution fusion | flops 1082130432 | bytes 12648448 | tf_op jit(solution)/shard_map/hclnr,hlocsr->holns/dot_general | solution.py:39
  412.9 6.6 %copy.35 = bf16[8,2,4,256,128]{4,3,2,1,0:T(8,128)(2,1)} copy(bf16[8,2,4,256,128]{3,4,1,2,0:T(8,128)(2,1)} %fusion.13) | data formatting | bytes 8388608 | tf_op jit(solution)/shard_map/convert_element_type | solution.py:40
  419.5 8.0 %fusion.65 = f32[64,256,128]{1,2,0:T(8,128)} fusion(bf16[64,256,128]{2,1,0:T(8,128)(2,1)} %bitcast.120, bf16[64,128,128]{1,2,0:T(8,128)(2,1)} %all-gather.9.cloned.1.call-done), kind=kOutput, calls=%fused_computation.62 | convolution fusion | flops 536870912 | bytes 14680064 | tf_op jit(solution)/shard_map/bmr,bcr->bmc/dot_general | solution.py:91
  427.5 37.7 %all-gather.11.cloned.1.call-done = bf16[64,2,128,128]{2,3,1,0:T(8,128)(2,1)} async-done(((bf16[64,2,128,64]{2,3,1,0:T(8,128)(2,1)}), bf16[64,2,128,128]{2,3,1,0:T(8,128)(2,1)}) %all-gather.11.cloned.1.call-update) | async-done | bytes 4194320 | tf_op jit(solution)/shard_map/all_gather | solution.py:65
  465.3 10.1 %fusion.6 = bf16[64,256,128]{1,2,0:T(8,128)(2,1)} fusion(f32[64,256,128]{1,2,0:T(8,128)} %fusion.65, bf16[64,2,128,128]{2,3,1,0:T(8,128)(2,1)} %all-gather.11.cloned.1.call-done, bf16[64,2,128,256]{3,2,1,0:T(8,128)(2,1)} %bitcast.116, pred[64,2]{1,0:T(8,128)(4,1)S(1)} %copy.36), kind=kOutput, calls=%fused_computation.16 | convolution fusion | flops 1082130432 | bytes 25165952 | tf_op jit(solution)/shard_map/bkmn,bknc->bmc/dot_general | solution.py:83
  (10 shorter events, 0.1 us)
Async XLA Ops:
  6.5 56.6 %all-gather.7.cloned.1.call-start = ((), (), s32[]{:S(2)}) async-start(), calls=%async_computation.3 | async-start | bytes 3145728 | tf_op jit(solution)/shard_map/all_gather | solution.py:63
  7.3 378.1 %all-gather.5.cloned.1.call-start = ((), (), s32[]{:S(2)}) async-start(), calls=%async_computation.2 | async-start | bytes 18874368 | tf_op jit(solution)/shard_map/all_gather | solution.py:71
  19.0 9.0 %copy-start.2 = (f32[3,32,2,2,128]{4,3,2,1,0:T(2,128)S(1)}, f32[3,32,2,2,128]{4,3,2,1,0:T(2,128)}, u32[]{:S(2)}) copy-start(f32[3,32,2,2,128]{4,3,2,1,0:T(2,128)} %param.15) | copy-start | bytes 589828
  19.0 260.1 %all-to-all-start = ((bf16[2,3,32,2,2,64,128]{6,5,4,3,2,1,0:T(8,128)(2,1)}), bf16[2,3,32,2,2,64,128]{6,5,4,3,2,1,0:T(8,128)(2,1)}, u32[]{:S(2)}, u32[]{:S(2)}) async-start(bf16[2,3,32,2,2,64,128]{6,5,4,3,2,1,0:T(8,128)(2,1)} %pad_maximum_fusion), calls=%async_computation | async-start | bytes 25165824 | tf_op jit(solution)/shard_map/all_to_all | solution.py:69
  285.7 7.9 %copy-start = (bf16[64,256,128]{2,1,0:T(8,128)(2,1)S(1)}, bf16[64,256,128]{2,1,0:T(8,128)(2,1)}, u32[]{:S(2)}) copy-start(bf16[64,256,128]{2,1,0:T(8,128)(2,1)} %convolution_convert_fusion) | copy-start | bytes 12582916
  320.0 19.2 %copy-start.3 = (f32[3,32,2,2,128]{4,3,2,1,0:T(2,128)S(1)}, f32[3,32,2,2,128]{4,3,2,1,0:T(2,128)}, u32[]{:S(2)}) copy-start(f32[3,32,2,2,128]{4,3,2,1,0:T(2,128)} %param.17) | copy-start | bytes 589828
  320.0 19.3 %copy-start.4 = (s32[64,2]{0,1:T(2,128)S(1)}, s32[64,2]{0,1:T(2,128)}, u32[]{:S(2)}) copy-start(s32[64,2]{0,1:T(2,128)} %param.13) | copy-start | bytes 1540
  320.0 71.6 %all-to-all-start.1 = ((bf16[64,256,128]{2,1,0:T(8,128)(2,1)}), bf16[64,256,128]{2,1,0:T(8,128)(2,1)}, u32[]{:S(2)}, u32[]{:S(2)}) async-start(bf16[64,256,128]{2,1,0:T(8,128)(2,1)} %bitcast.121), calls=%async_computation.1 | async-start | bytes 8388608 | tf_op jit(solution)/shard_map/all_to_all | solution.py:86
  331.2 88.3 %all-gather.9.cloned.1.call-start = ((), (), s32[]{:S(2)}) async-start(), calls=%async_computation.4 | async-start | bytes 3145728 | tf_op jit(solution)/shard_map/all_gather | solution.py:64
  331.9 133.3 %all-gather.11.cloned.1.call-start = ((), (), s32[]{:S(2)}) async-start(), calls=%async_computation.5 | async-start | bytes 6291456 | tf_op jit(solution)/shard_map/all_gather | solution.py:65
  333.5 39.0 %collective-permute-start = (bf16[2,128,256]{2,1,0:T(8,128)(2,1)S(1)}, bf16[2,128,256]{2,1,0:T(8,128)(2,1)S(1)}, u32[]{:S(2)}, u32[]{:S(2)}) collective-permute-start(bf16[2,128,256]{2,1,0:T(8,128)(2,1)S(1)} %bitcast.132), channel_id=1, source_target_pairs={{0,2},{2,4},{4,6},{6,8},{8,10},{10,12},{12,14},{14,16},{16,18},{18... | collective-permute-start | bytes 393224 | tf_op jit(solution)/shard_map/ppermute | solution.py:19
  337.1 35.4 %collective-permute-start.1 = (bf16[2,128,256]{2,1,0:T(8,128)(2,1)S(1)}, bf16[2,128,256]{2,1,0:T(8,128)(2,1)S(1)}, u32[]{:S(2)}, u32[]{:S(2)}) collective-permute-start(bf16[2,128,256]{2,1,0:T(8,128)(2,1)S(1)} %bitcast.131), channel_id=1, source_target_pairs={{2,0},{4,2},{6,4},{8,6},{10,8},{12,10},{14,12},{16,14},{18,16},{20... | collective-permute-start | bytes 393224 | tf_op jit(solution)/shard_map/ppermute | solution.py:21
  391.6 4.9 %copy-start.1 = (bf16[1,32,2,2,128,128]{5,4,3,2,1,0:T(8,128)(2,1)S(1)}, bf16[1,32,2,2,128,128]{5,4,3,2,1,0:T(8,128)(2,1)}, u32[]{:S(2)}) copy-start(bf16[1,32,2,2,128,128]{5,4,3,2,1,0:T(8,128)(2,1)} %get-tuple-element.8) | copy-start | bytes 12582916
Sparse Core Ops, SparseCore 0:
  9.0 54.0 all-gather.6
  64.8 252.7 all-gather.4
  333.7 69.2 all-gather.8
  404.5 60.7 all-gather.10
